TPU v7x, 256 devices: a whole 4x4x8 slice. The times are simulated.
256 devices in a mesh: ctx: 8 (over x, y_hi), chan: 32 (over z, y_lo, core).
Axes of the slice: x: 4, y: 4 (y_hi: 2, y_lo: 2; y = y_hi * 2 + y_lo), z: 8, core: 2. Of those that a mesh axis runs over, the one named last changes fastest.
Arguments:
- inputs: bfloat16 [4096, 4096], P('ctx', 'chan'), may hold values from -6 to 6
- w_in: bfloat16 [4096, 3, 4096], P(None, None, 'chan'), may hold values from -0.09375 to 0.09375
- conv_taps: bfloat16 [3, 3, 4096], P(None, None, 'chan'), may hold values from -3.59375 to 3.59375
- skip_gain: float32 [4096], P('chan'), may hold values from 0.5 to 1.5
- filter_taps: bfloat16 [4096, 4096], P('ctx', 'chan'), may hold values from -0.09375 to 0.09375
- w_out: bfloat16 [4096, 4096], P('chan'), may hold values from -0.1875 to 0.1875
Outputs:
- result: bfloat16 [4096, 4096], P('ctx', 'chan')
All inputs are finite; a program needn't handle non-finite values.
Results may differ from a plain program's by a relative error of at most 0.024.
Values may be sent and summed in bfloat16 or wider, within the bound.
A program may use at most 64 MiB of HBM per device.

v0:
```python
import math
import jax
import jax.numpy as jnp
from jax import lax
from jax.sharding import PartitionSpec as P

KERNEL = 3


def dft_table(double_len):
    step = 32
    hi_ids = jnp.arange(double_len // step, dtype=jnp.int32)[:, None]
    lo_ids = jnp.arange(step, dtype=jnp.int32)[:, None]
    cols = jnp.arange(double_len, dtype=jnp.int32)[None, :]
    scale = 2.0 * math.pi / double_len
    hi_angle = scale * (hi_ids * step * cols % double_len).astype(jnp.float32)
    lo_angle = scale * (lo_ids * cols % double_len).astype(jnp.float32)
    hc, hs = (jnp.cos(hi_angle)[:, None], jnp.sin(hi_angle)[:, None])
    lc, ls = (jnp.cos(lo_angle)[None], jnp.sin(lo_angle)[None])
    cos = (hc * lc - hs * ls).reshape(double_len, double_len)
    sin = (hs * lc + hc * ls).reshape(double_len, double_len)
    return jnp.concatenate([cos, -sin], 0).astype(jnp.bfloat16)


def body(inputs, w_in, conv_taps, skip_gain, filter_taps, w_out):
    span_len, width_dev = inputs.shape
    double_len = 2 * span_len
    groups = lax.axis_size("ctx")
    position = lax.axis_index("ctx")
    own = width_dev // groups
    with jax.named_scope("out_weight_columns"):
        w_cols = lax.all_to_all(w_out, "chan", 1, 0, tiled=True)
    with jax.named_scope("filter_to_owner"):
        taps_t = filter_taps.T.reshape(groups, own, span_len)
        taps_t = lax.all_to_all(taps_t, "ctx", 0, 0, tiled=True)
    with jax.named_scope("input_projection"):
        inputs_t = lax.all_gather(inputs.T, "chan", axis=0, tiled=True)
        w_flat = w_in.reshape(w_in.shape[0], 3 * width_dev)
        proj_t = lax.dot_general(
            w_flat, inputs_t, (((0,), (0,)), ((), ())), preferred_element_type=jnp.float32
        ).astype(jnp.bfloat16)
    with jax.named_scope("projection_to_owner"):
        proj_t = proj_t.reshape(3, groups, own, span_len)
        proj_t = lax.all_to_all(proj_t, "ctx", 1, 1, tiled=True)
    with jax.named_scope("short_conv"):
        start = position * own
        taps = lax.dynamic_slice_in_dim(conv_taps, start, own, axis=2)
        rim = jnp.pad(
            proj_t[:, :-1, :, span_len - (KERNEL - 1) :], ((0, 0), (1, 0), (0, 0), (0, 0))
        )
        padded = jnp.concatenate([rim, proj_t], 3)
        filtered = jnp.zeros(proj_t.shape, jnp.float32)
        for lag in range(KERNEL):
            start_row = KERNEL - 1 - lag
            filtered = filtered + taps[lag].astype(jnp.float32)[:, None, :, None] * padded[
                ..., start_row : start_row + span_len
            ].astype(jnp.float32)
        streams = filtered.astype(jnp.bfloat16)
        gate_out = streams[0]
        gated_in = (streams[1].astype(jnp.float32) * streams[2].astype(jnp.float32)).astype(
            jnp.bfloat16
        )
    with jax.named_scope("spectra"):
        table = dft_table(double_len)
        forward_in = table[:, :span_len]
        spectra_in = jnp.einsum(
            "jdb,fb->jdf", gated_in, forward_in, preferred_element_type=jnp.float32
        ).astype(jnp.bfloat16)
        previous = jnp.pad(taps_t[:-1, :, 1:], ((1, 0), (0, 0), (0, 0)))
        padded_taps = jnp.concatenate(
            [taps_t, jnp.zeros((groups, own, 1), jnp.bfloat16), previous], 2
        )
        spectra_taps = jnp.einsum(
            "kdm,fm->kdf", padded_taps, table, preferred_element_type=jnp.float32
        ).astype(jnp.bfloat16)
    with jax.named_scope("mixture"):
        real_g = spectra_taps[:, :, :double_len].astype(jnp.float32)
        imag_g = spectra_taps[:, :, double_len:].astype(jnp.float32)
        real_u = spectra_in[:, :, :double_len].astype(jnp.float32)
        imag_u = spectra_in[:, :, double_len:].astype(jnp.float32)
        mixed = []
        for target in range(groups):
            acc_r = jnp.zeros((own, double_len), jnp.float32)
            acc_i = jnp.zeros((own, double_len), jnp.float32)
            for source in range(target + 1):
                lag = target - source
                acc_r = acc_r + (real_g[lag] * real_u[source] - imag_g[lag] * imag_u[source])
                acc_i = acc_i + (real_g[lag] * imag_u[source] + imag_g[lag] * real_u[source])
            mixed.append(jnp.concatenate([acc_r, acc_i], 1))
        mixture = jnp.stack(mixed, 0).astype(jnp.bfloat16)
    with jax.named_scope("inverse_and_gate"):
        long_out = jnp.einsum(
            "idf,fa->ida", mixture, forward_in, preferred_element_type=jnp.float32
        ) * (1.0 / double_len)
        gain = lax.dynamic_slice_in_dim(skip_gain, start, own)
        long_out = long_out + gain[None, :, None] * gated_in.astype(jnp.float32)
        gated_out = (gate_out.astype(jnp.float32) * long_out).astype(jnp.bfloat16)
    with jax.named_scope("gated_back_to_rows"):
        gated_out = lax.all_to_all(gated_out, "ctx", 0, 0, tiled=True)
        gated_out = gated_out.reshape(width_dev, span_len)
    with jax.named_scope("output_projection"):
        gathered = lax.all_gather(gated_out, "chan", axis=0, tiled=True)
        result = lax.dot_general(
            gathered, w_cols, (((0,), (0,)), ((), ())), preferred_element_type=jnp.float32
        ).astype(jnp.bfloat16)
    return result


def solution(mesh):
    return jax.shard_map(
        body,
        mesh=mesh,
        in_specs=(
            P("ctx", "chan"),
            P(None, None, "chan"),
            P(None, None, "chan"),
            P("chan"),
            P("ctx", "chan"),
            P("chan", None),
        ),
        out_specs=P("ctx", "chan"),
        check_vma=False,
    )
```

profile of v0, /device:TPU:1, one launch (start us, length us, event | category | flops | bytes accessed | tf_op | source)
XLA Modules:
  0.0 208.1 jit_solution(4928286048202900547)
XLA Ops:
  6.5 0.7 all-gather.3.cloned.1.call-update
  7.3 1.9 copy.19
  9.1 7.5 %all-to-all-start.1 = ((bf16[8,16,512]{2,1,0:T(8,128)(2,1)}), bf16[8,16,512]{2,1,0:T(8,128)(2,1)S(1)}, u32[]{:S(2)}, u32[]{:S(2)}) async-start(bf16[8,16,512]{2,1,0:T(8,128)(2,1)} %bitcast.8), calls=%async_computation.1 | async-start | bytes 262144 | tf_op jit(solution)/shard_map/filter_to_owner/all_to_all | solution.py:35
  16.6 0.5 fusion.45
  17.2 0.6 fusion.48
  17.8 3.5 %negate_convert_fusion = (bf16[32,32,1024]{2,1,0:T(8,128)(2,1)}, bf16[32,32,1024]{2,1,0:T(8,128)(2,1)}) fusion(f32[32,1024]{1,0:T(8,128)S(1)} %get-tuple-element.22, f32[32,1024]{1,0:T(8,128)S(1)} %get-tuple-element.21, f32[32,1024]{1,0:T(8,128)S(1)} %get-tuple-element.23, f32[32,1024]{1,0:T(8,128)S(1)} %get-tuple-element.20), kind=kLoop, calls=%fused_computation.5 | loop fusion | flops 9437184 | bytes 4718592 | tf_op jit(solution)/shard_map/convert.44
  21.3 2.9 %copy.14 = bf16[4096,3,128]{0,2,1:T(8,128)(2,1)} copy(bf16[4096,3,128]{2,0,1:T(8,128)(2,1)S(1)} %copy-done) | data formatting | bytes 6291456 | tf_op args[1]
  24.5 61.2 %all-gather.3.cloned.1.call-done = bf16[4096,512]{0,1:T(8,128)(2,1)} async-done(((bf16[128,512]{0,1:T(8,128)(2,1)}), bf16[4096,512]{0,1:T(8,128)(2,1)}) %all-gather.3.cloned.1.call-update) | async-done | bytes 4194320 | tf_op jit(solution)/shard_map/input_projection/all_gather | solution.py:37
  85.6 5.1 %convolution_convert_fusion.1 = bf16[384,512]{1,0:T(8,128)(2,1)S(1)} fusion(bf16[4096,384]{0,1:T(8,128)(2,1)} %bitcast.117, bf16[4096,512]{0,1:T(8,128)(2,1)} %all-gather.3.cloned.1.call-done), kind=kOutput, calls=%fused_computation.11 | convolution fusion | flops 1610809344 | bytes 7733248 | tf_op jit(solution)/shard_map/input_projection/dot_general | solution.py:39
  90.7 0.8 copy.15
  91.5 6.4 %all-to-all-start = ((bf16[3,8,16,512]{3,2,0,1:T(8,128)(2,1)}), bf16[3,8,16,512]{3,2,0,1:T(8,128)(2,1)S(1)}, u32[]{:S(2)}, u32[]{:S(2)}) async-start(bf16[3,8,16,512]{3,2,0,1:T(8,128)(2,1)} %copy.15), calls=%async_computation | async-start | bytes 786432 | tf_op jit(solution)/shard_map/projection_to_owner/all_to_all | solution.py:44
  97.9 3.2 %fusion.3 = bf16[8,16,2048]{2,1,0:T(8,128)(2,1)S(1)} fusion(bf16[1024,1024]{1,0:T(8,128)(2,1)S(1)} %bitcast.118, bf16[1024,1024]{1,0:T(8,128)(2,1)} %bitcast.121, bf16[7,16,511]{2,1,0:T(8,128)(2,1)S(1)} %slice.145, bf16[8,16,512]{2,1,0:T(8,128)(2,1)} %copy-done.4, bf16[1024]{0:T(1024)(128)(2,1)S(1)} %pad.29.clone), kind=kOutput, calls=%fused_computation.7 | convolution fusion | flops 546570240 | bytes 4966176 | tf_op jit(solution)/shard_map/spectra/kdm,fm->kdf/dot_general | solution.py:73
  101.1 0.1 slice_convert_fusion.3
  101.2 6.1 %all-to-all-done = bf16[3,8,16,512]{3,2,0,1:T(8,128)(2,1)S(1)} async-done(((bf16[3,8,16,512]{3,2,0,1:T(8,128)(2,1)}), bf16[3,8,16,512]{3,2,0,1:T(8,128)(2,1)S(1)}, u32[]{:S(2)}, u32[]{:S(2)}) %all-to-all-start) | async-done | bytes 393248 | tf_op jit(solution)/shard_map/projection_to_owner/all_to_all | solution.py:44
  107.4 0.2 fusion.13
  107.7 0.4 add_convert_fusion
  108.0 2.0 convolution_convert_fusion
  110.1 0.1 slice_convert_fusion.2
  110.2 0.2 fusion.63
  110.4 0.2 fusion.64
  110.5 0.1 fusion.61
  110.7 0.1 fusion.62
  110.8 0.1 fusion.59
  110.9 0.1 fusion.60
  111.7 1.0 copy-done.2
  112.6 0.5 fusion.10
  113.1 9.8 %all_to_all.34 = bf16[8,16,512]{2,1,0:T(8,128)(2,1)} all-to-all(bf16[8,16,512]{2,1,0:T(8,128)(2,1)S(1)} %fusion.10), channel_id=1, replica_groups=mesh['ctx'=8,'chan'=32] {'ctx'}, dimensions={0} | all-to-all | bytes 262144 | tf_op jit(solution)/shard_map/gated_back_to_rows/all_to_all | solution.py:99
  123.0 0.7 copy.20
  123.7 44.2 %all_to_all.35 = bf16[128,32,128]{0,2,1:T(8,128)(2,1)S(1)} all-to-all(bf16[128,32,128]{0,2,1:T(8,128)(2,1)S(1)} %bitcast.116), channel_id=1, replica_groups=mesh['ctx'=8,'chan'=32] {'chan'}, dimensions={1} | all-to-all | bytes 2097152 | tf_op jit(solution)/shard_map/out_weight_columns/all_to_all | solution.py:32
  167.9 0.7 copy.21
  168.6 28.6 %all-gather.5.cloned.1.call-done = bf16[4096,512]{1,0:T(8,128)(2,1)} async-done(((bf16[128,512]{1,0:T(8,128)(2,1)}), bf16[4096,512]{1,0:T(8,128)(2,1)}) %all-gather.5.cloned.1.call-update) | async-done | bytes 4194320 | tf_op jit(solution)/shard_map/output_projection/all_gather | solution.py:102
  197.1 4.1 %convolution_convert_fusion.2 = bf16[512,128]{1,0:T(8,128)(2,1)} fusion(bf16[4096,512]{1,0:T(8,128)(2,1)} %all-gather.5.cloned.1.call-done, bf16[4096,128]{1,0:T(8,128)(2,1)S(1)} %bitcast.124), kind=kOutput, calls=%fused_computation.15 | convolution fusion | flops 536936448 | bytes 5373952 | tf_op jit(solution)/shard_map/output_projection/dot_general | solution.py:103
  (39 shorter events, 0.9 us)
Async XLA Ops:
  6.5 14.8 %copy-start = (bf16[4096,3,128]{2,0,1:T(8,128)(2,1)S(1)}, bf16[4096,3,128]{2,0,1:T(8,128)(2,1)}, u32[]{:S(2)}) copy-start(bf16[4096,3,128]{2,0,1:T(8,128)(2,1)} %param.7) | copy-start | bytes 9437188
  6.5 79.1 %all-gather.3.cloned.1.call-start = ((), (), s32[]{:S(2)}) async-start(), calls=%async_computation.4 | async-start | bytes 4325376 | tf_op jit(solution)/shard_map/input_projection/all_gather | solution.py:37
  9.1 15.2 %all-to-all-start.1 = ((bf16[8,16,512]{2,1,0:T(8,128)(2,1)}), bf16[8,16,512]{2,1,0:T(8,128)(2,1)S(1)}, u32[]{:S(2)}, u32[]{:S(2)}) async-start(bf16[8,16,512]{2,1,0:T(8,128)(2,1)} %bitcast.8), calls=%async_computation.1 | async-start | bytes 262144 | tf_op jit(solution)/shard_map/filter_to_owner/all_to_all | solution.py:35
  21.3 2.9 %copy-start.6 = (f32[128]{0:T(128)S(1)}, f32[128]{0:T(128)}, u32[]{:S(2)}) copy-start(f32[128]{0:T(128)} %param.9) | copy-start | bytes 1540
  21.3 3.0 %copy-start.5 = (bf16[3,3,128]{2,1,0:T(4,128)(2,1)S(1)}, bf16[3,3,128]{2,1,0:T(4,128)(2,1)}, u32[]{:S(2)}) copy-start(bf16[3,3,128]{2,1,0:T(4,128)(2,1)} %param.8) | copy-start | bytes 6916
  24.4 66.4 %copy-start.4 = (bf16[8,16,512]{2,1,0:T(8,128)(2,1)}, bf16[8,16,512]{2,1,0:T(8,128)(2,1)S(1)}, u32[]{:S(2)}) copy-start(bf16[8,16,512]{2,1,0:T(8,128)(2,1)S(1)} %all-to-all-done.1) | copy-start | bytes 393220
  85.6 12.3 %copy-start.1 = (bf16[32,32,1024]{2,1,0:T(8,128)(2,1)S(1)}, bf16[32,32,1024]{2,1,0:T(8,128)(2,1)}, u32[]{:S(2)}) copy-start(bf16[32,32,1024]{2,1,0:T(8,128)(2,1)} %get-tuple-element.15) | copy-start | bytes 6291460
  91.5 15.8 %all-to-all-start = ((bf16[3,8,16,512]{3,2,0,1:T(8,128)(2,1)}), bf16[3,8,16,512]{3,2,0,1:T(8,128)(2,1)S(1)}, u32[]{:S(2)}, u32[]{:S(2)}) async-start(bf16[3,8,16,512]{3,2,0,1:T(8,128)(2,1)} %copy.15), calls=%async_computation | async-start | bytes 786432 | tf_op jit(solution)/shard_map/projection_to_owner/all_to_all | solution.py:44
  97.9 99.3 %all-gather.5.cloned.1.call-start = ((), (), s32[]{:S(2)}) async-start(), calls=%async_computation.5 | async-start | bytes 4325376 | tf_op jit(solution)/shard_map/output_projection/all_gather | solution.py:102
  111.1 1.6 copy-start.2
  111.5 11.4 %copy-start.3 = (bf16[128,4096]{1,0:T(8,128)(2,1)S(1)}, bf16[128,4096]{1,0:T(8,128)(2,1)}, u32[]{:S(2)}) copy-start(bf16[128,4096]{1,0:T(8,128)(2,1)} %param.11) | copy-start | bytes 3145732
Sparse Core Ops, SparseCore 0:
  9.1 76.4 all-gather.2
  123.1 74.0 all-gather.4
where the time goes:
time: 209 us; the launch traced here: 208 us
  waiting for transfers between devices  96.6 us (46%)
  blocking collectives  54.1 us (26%)
  matrix products  14.9 us (7%)
  starting transfers between devices  13.9 us (7%)
  between operations  13.7 us (7%)
  local copies, waits for them, and re-layouts  8.15 us (4%)
  other arithmetic  6.84 us (3%)
    all_gather x1, waiting for transfers between devices, body(): inputs_t = lax.all_gather(inputs.T, 'chan', axis=0, tiled=True)  61.2 us
    all_to_all x1, blocking collectives, body(): w_cols = lax.all_to_all(w_out, 'chan', 1, 0, tiled=True)  44.2 us
    all_gather x1, waiting for transfers between devices, body(): gathered = lax.all_gather(gated_out, 'chan', axis=0, tiled=True)  28.6 us
    all_to_all x1, blocking collectives, body(): gated_out = lax.all_to_all(gated_out, 'ctx', 0, 0, tiled=True)  9.83 us
    all_to_all x1, starting transfers between devices, body(): taps_t = lax.all_to_all(taps_t, 'ctx', 0, 0, tiled=True)  7.48 us
    all_to_all x1, starting transfers between devices, body(): proj_t = lax.all_to_all(proj_t, 'ctx', 1, 1, tiled=True)  6.35 us
    all_to_all x1, waiting for transfers between devices, body(): proj_t = lax.all_to_all(proj_t, 'ctx', 1, 1, tiled=True)  6.07 us
    dot_general x1, matrix products, body(): lax.dot_general(w_flat, inputs_t, (((0,), (0,)), ((), ())), preferred_ele...  5.1 us
  transfers between devices with their start and end apart: 4, of which 3 were waited for; matrix products, arithmetic and copies ran while one was open for 7% of the time, Pallas kernels for 0%

commit v1 on v0

--- a/solution.py
+++ b/solution.py
@@ -29,7 +29,12 @@
     position = lax.axis_index("ctx")
     own = width_dev // groups
     with jax.named_scope("out_weight_columns"):
-        w_cols = lax.all_to_all(w_out, "chan", 1, 0, tiled=True)
+        w_cols = jnp.concatenate(
+            lax.all_to_all(
+                jnp.stack(jnp.split(w_out, lax.axis_size("chan"), axis=1)), "chan", 0, 0
+            ),
+            axis=0,
+        )
     with jax.named_scope("filter_to_owner"):
         taps_t = filter_taps.T.reshape(groups, own, span_len)
         taps_t = lax.all_to_all(taps_t, "ctx", 0, 0, tiled=True)

time: 209 us -> 211 us (level)
  local copies, waits for them, and re-layouts: 8.15 us -> 29.7 us
  waiting for transfers between devices: 96.6 us -> 83.6 us
  blocking collectives: 54.1 us -> 43.3 us
  starting transfers between devices: 13.9 us -> 17.2 us
    unnamed x17 -> x49, local copies, waits for them, and re-layouts: 4.57 us -> 26.1 us
    all_gather x1, waiting for transfers between devices: 28.6 us -> 13.7 us  [body(): gathered = lax.all_gather(gated_out, 'chan', axis=0, tiled=True)]
    all_to_all x2 -> x1, blocking collectives: 54.1 us -> 43.3 us  [body(): lax.all_to_all(jnp.stack(jnp.split(w_out, lax.axis_size('chan'), axis=1))...]
    all_to_all x0 -> x1, waiting for transfers between devices: none -> 6.03 us  [body(): gated_out = lax.all_to_all(gated_out, 'ctx', 0, 0, tiled=True)]
    all_gather x1, waiting for transfers between devices: 61.2 us -> 57 us  [body(): inputs_t = lax.all_gather(inputs.T, 'chan', axis=0, tiled=True)]
    all_to_all x0 -> x1, starting transfers between devices: none -> 3.37 us  [body(): gated_out = lax.all_to_all(gated_out, 'ctx', 0, 0, tiled=True)]
  transfers between devices with their start and end apart: 4 -> 5, of which waited for: 3 -> 4; matrix products, arithmetic and copies ran while one was open for 7% -> 17% of each run, Pallas kernels for 0% -> 0%
where the time goes in v1:
time: 211 us; the launch traced here: 210 us
  waiting for transfers between devices  83.6 us (40%)
  blocking collectives  43.3 us (21%)
  local copies, waits for them, and re-layouts  29.7 us (14%)
  starting transfers between devices  17.2 us (8%)
  matrix products  15.6 us (7%)
  between operations  13.7 us (6%)
  other arithmetic  6.83 us (3%)
    all_gather x1, waiting for transfers between devices, body(): inputs_t = lax.all_gather(inputs.T, 'chan', axis=0, tiled=True)  57 us
    all_to_all x1, blocking collectives, body(): lax.all_to_all(jnp.stack(jnp.split(w_out, lax.axis_size('chan'), axis=1))...  43.3 us
    unnamed x49, local copies, waits for them, and re-layouts  26.1 us
    all_gather x1, waiting for transfers between devices, body(): gathered = lax.all_gather(gated_out, 'chan', axis=0, tiled=True)  13.7 us
    all_to_all x1, starting transfers between devices, body(): taps_t = lax.all_to_all(taps_t, 'ctx', 0, 0, tiled=True)  7.48 us
    all_to_all x1, starting transfers between devices, body(): proj_t = lax.all_to_all(proj_t, 'ctx', 1, 1, tiled=True)  6.35 us
    all_to_all x1, waiting for transfers between devices, body(): proj_t = lax.all_to_all(proj_t, 'ctx', 1, 1, tiled=True)  6.12 us
    all_to_all x1, waiting for transfers between devices, body(): gated_out = lax.all_to_all(gated_out, 'ctx', 0, 0, tiled=True)  6.03 us
  transfers between devices with their start and end apart: 5, of which 4 were waited for; matrix products, arithmetic and copies ran while one was open for 17% of the time, Pallas kernels for 0%

profile of v1, /device:TPU:1, one launch (start us, length us, event | category | flops | bytes accessed | tf_op | source)
XLA Modules:
  0.0 210.0 jit_solution(15848799606438609231)
XLA Ops:
  6.5 0.7 all-gather.3.cloned.1.call-update
  7.3 1.9 copy.15
  9.1 7.5 %all-to-all-start.1 = ((bf16[8,16,512]{2,1,0:T(8,128)(2,1)}), bf16[8,16,512]{2,1,0:T(8,128)(2,1)S(1)}, u32[]{:S(2)}, u32[]{:S(2)}) async-start(bf16[8,16,512]{2,1,0:T(8,128)(2,1)} %bitcast.8), calls=%async_computation.1 | async-start | bytes 262144 | tf_op jit(solution)/shard_map/filter_to_owner/all_to_all | solution.py:40
  17.2 1.4 constant_dynamic-update-slice_fusion.39
  18.5 1.4 constant_dynamic-update-slice_fusion.38
  20.5 3.5 %negate_convert_fusion = (bf16[32,32,1024]{2,1,0:T(8,128)(2,1)}, bf16[32,32,1024]{2,1,0:T(8,128)(2,1)}) fusion(f32[32,1024]{1,0:T(8,128)S(1)} %get-tuple-element.22, f32[32,1024]{1,0:T(8,128)S(1)} %get-tuple-element.21, f32[32,1024]{1,0:T(8,128)S(1)} %get-tuple-element.23, f32[32,1024]{1,0:T(8,128)S(1)} %get-tuple-element.20), kind=kLoop, calls=%fused_computation.5 | loop fusion | flops 9437184 | bytes 4718592 | tf_op jit(solution)/shard_map/convert.44
  24.0 1.4 constant_dynamic-update-slice_fusion.37
  25.4 2.9 %copy.10 = bf16[4096,3,128]{0,2,1:T(8,128)(2,1)} copy(bf16[4096,3,128]{2,0,1:T(8,128)(2,1)S(1)} %copy-done) | data formatting | bytes 6291456 | tf_op args[1]
  28.6 57.0 %all-gather.3.cloned.1.call-done = bf16[4096,512]{0,1:T(8,128)(2,1)} async-done(((bf16[128,512]{0,1:T(8,128)(2,1)}), bf16[4096,512]{0,1:T(8,128)(2,1)}) %all-gather.3.cloned.1.call-update) | async-done | bytes 4194320 | tf_op jit(solution)/shard_map/input_projection/all_gather | solution.py:42
  85.6 5.1 %convolution_convert_fusion.1 = bf16[384,512]{1,0:T(8,128)(2,1)S(1)} fusion(bf16[4096,384]{0,1:T(8,128)(2,1)} %bitcast.177, bf16[4096,512]{0,1:T(8,128)(2,1)} %all-gather.3.cloned.1.call-done), kind=kOutput, calls=%fused_computation.11 | convolution fusion | flops 1610809344 | bytes 7733248 | tf_op jit(solution)/shard_map/input_projection/dot_general | solution.py:44
  90.7 0.8 copy.11
  91.5 6.4 %all-to-all-start = ((bf16[3,8,16,512]{3,2,0,1:T(8,128)(2,1)}), bf16[3,8,16,512]{3,2,0,1:T(8,128)(2,1)S(1)}, u32[]{:S(2)}, u32[]{:S(2)}) async-start(bf16[3,8,16,512]{3,2,0,1:T(8,128)(2,1)} %copy.11), calls=%async_computation | async-start | bytes 786432 | tf_op jit(solution)/shard_map/projection_to_owner/all_to_all | solution.py:49
  97.9 3.2 %fusion.3 = bf16[8,16,2048]{2,1,0:T(8,128)(2,1)S(1)} fusion(bf16[1024,1024]{1,0:T(8,128)(2,1)S(1)} %bitcast.178, bf16[1024,1024]{1,0:T(8,128)(2,1)} %bitcast.181, bf16[7,16,511]{2,1,0:T(8,128)(2,1)S(1)} %slice.145, bf16[8,16,512]{2,1,0:T(8,128)(2,1)} %copy-done.5, bf16[1024]{0:T(1024)(128)(2,1)S(1)} %pad.29.clone), kind=kOutput, calls=%fused_computation.7 | convolution fusion | flops 546570240 | bytes 4966176 | tf_op jit(solution)/shard_map/spectra/kdm,fm->kdf/dot_general | solution.py:78
  101.2 6.1 %all-to-all-done = bf16[3,8,16,512]{3,2,0,1:T(8,128)(2,1)S(1)} async-done(((bf16[3,8,16,512]{3,2,0,1:T(8,128)(2,1)}), bf16[3,8,16,512]{3,2,0,1:T(8,128)(2,1)S(1)}, u32[]{:S(2)}, u32[]{:S(2)}) %all-to-all-start) | async-done | bytes 393248 | tf_op jit(solution)/shard_map/projection_to_owner/all_to_all | solution.py:49
  108.0 2.0 convolution_convert_fusion
  111.7 1.0 copy-done.2
  112.7 1.1 fusion.10
  113.8 3.4 %all-to-all-start.2 = ((bf16[8,16,512]{2,1,0:T(8,128)(2,1)}), bf16[8,16,512]{2,1,0:T(8,128)(2,1)S(1)}, u32[]{:S(2)}, u32[]{:S(2)}) async-start(bf16[8,16,512]{2,1,0:T(8,128)(2,1)} %fusion.10), calls=%async_computation.2 | async-start | bytes 262144 | tf_op jit(solution)/shard_map/gated_back_to_rows/all_to_all | solution.py:104
  117.8 6.0 %all-to-all-done.2 = bf16[8,16,512]{2,1,0:T(8,128)(2,1)S(1)} async-done(((bf16[8,16,512]{2,1,0:T(8,128)(2,1)}), bf16[8,16,512]{2,1,0:T(8,128)(2,1)S(1)}, u32[]{:S(2)}, u32[]{:S(2)}) %all-to-all-start.2) | async-done | bytes 131104 | tf_op jit(solution)/shard_map/gated_back_to_rows/all_to_all | solution.py:104
  123.9 0.7 copy-done.4
  127.6 0.6 constant_dynamic-update-slice_fusion.30
  130.7 0.6 constant_dynamic-update-slice_fusion.25
  131.4 0.6 constant_dynamic-update-slice_fusion.24
  132.0 0.6 constant_dynamic-update-slice_fusion.23
  133.2 0.6 constant_dynamic-update-slice_fusion.21
  134.5 0.6 constant_dynamic-update-slice_fusion.19
  137.6 0.6 constant_dynamic-update-slice_fusion.14
  140.1 0.6 constant_dynamic-update-slice_fusion.10
  140.7 0.6 constant_dynamic-update-slice_fusion.9
  142.0 43.3 %all_to_all.20 = bf16[32,128,128]{2,1,0:T(8,128)(2,1)S(1)} all-to-all(bf16[32,128,128]{2,1,0:T(8,128)(2,1)} %constant_dynamic-update-slice_fusion.8), channel_id=1, replica_groups=mesh['ctx'=8,'chan'=32] {'chan'}, dimensions={0} | all-to-all | bytes 2097152 | tf_op jit(solution)/shard_map/out_weight_columns/all_to_all | solution.py:33
  185.3 13.7 %all-gather.5.cloned.1.call-done = bf16[4096,512]{1,0:T(8,128)(2,1)} async-done(((bf16[128,512]{1,0:T(8,128)(2,1)}), bf16[4096,512]{1,0:T(8,128)(2,1)}) %all-gather.5.cloned.1.call-update) | async-done | bytes 4194320 | tf_op jit(solution)/shard_map/output_projection/all_gather | solution.py:107
  199.0 4.1 %convolution_convert_fusion.2 = bf16[512,128]{1,0:T(8,128)(2,1)} fusion(bf16[4096,512]{1,0:T(8,128)(2,1)} %all-gather.5.cloned.1.call-done, bf16[4096,128]{1,0:T(8,128)(2,1)S(1)} %bitcast.184), kind=kOutput, calls=%fused_computation.15 | convolution fusion | flops 536936448 | bytes 5373952 | tf_op jit(solution)/shard_map/output_projection/dot_general | solution.py:108
  (72 shorter events, 16.1 us)
Async XLA Ops:
  6.5 18.9 %copy-start = (bf16[4096,3,128]{2,0,1:T(8,128)(2,1)S(1)}, bf16[4096,3,128]{2,0,1:T(8,128)(2,1)}, u32[]{:S(2)}) copy-start(bf16[4096,3,128]{2,0,1:T(8,128)(2,1)} %param.7) | copy-start | bytes 9437188
  6.5 79.1 %all-gather.3.cloned.1.call-start = ((), (), s32[]{:S(2)}) async-start(), calls=%async_computation.4 | async-start | bytes 4325376 | tf_op jit(solution)/shard_map/input_projection/all_gather | solution.py:42
  9.1 19.4 %all-to-all-start.1 = ((bf16[8,16,512]{2,1,0:T(8,128)(2,1)}), bf16[8,16,512]{2,1,0:T(8,128)(2,1)S(1)}, u32[]{:S(2)}, u32[]{:S(2)}) async-start(bf16[8,16,512]{2,1,0:T(8,128)(2,1)} %bitcast.8), calls=%async_computation.1 | async-start | bytes 262144 | tf_op jit(solution)/shard_map/filter_to_owner/all_to_all | solution.py:40
  24.0 4.3 %copy-start.7 = (f32[128]{0:T(128)S(1)}, f32[128]{0:T(128)}, u32[]{:S(2)}) copy-start(f32[128]{0:T(128)} %param.9) | copy-start | bytes 1540
  24.0 4.4 %copy-start.6 = (bf16[3,3,128]{2,1,0:T(4,128)(2,1)S(1)}, bf16[3,3,128]{2,1,0:T(4,128)(2,1)}, u32[]{:S(2)}) copy-start(bf16[3,3,128]{2,1,0:T(4,128)(2,1)} %param.8) | copy-start | bytes 6916
  28.5 62.2 %copy-start.5 = (bf16[8,16,512]{2,1,0:T(8,128)(2,1)}, bf16[8,16,512]{2,1,0:T(8,128)(2,1)S(1)}, u32[]{:S(2)}) copy-start(bf16[8,16,512]{2,1,0:T(8,128)(2,1)S(1)} %all-to-all-done.1) | copy-start | bytes 393220
  85.6 12.3 %copy-start.1 = (bf16[32,32,1024]{2,1,0:T(8,128)(2,1)S(1)}, bf16[32,32,1024]{2,1,0:T(8,128)(2,1)}, u32[]{:S(2)}) copy-start(bf16[32,32,1024]{2,1,0:T(8,128)(2,1)} %get-tuple-element.15) | copy-start | bytes 6291460
  91.5 15.8 %all-to-all-start = ((bf16[3,8,16,512]{3,2,0,1:T(8,128)(2,1)}), bf16[3,8,16,512]{3,2,0,1:T(8,128)(2,1)S(1)}, u32[]{:S(2)}, u32[]{:S(2)}) async-start(bf16[3,8,16,512]{3,2,0,1:T(8,128)(2,1)} %copy.11), calls=%async_computation | async-start | bytes 786432 | tf_op jit(solution)/shard_map/projection_to_owner/all_to_all | solution.py:49
  111.1 1.6 copy-start.2
  111.5 5.7 %copy-start.3 = (bf16[128,4096]{1,0:T(8,128)(2,1)S(1)}, bf16[128,4096]{1,0:T(8,128)(2,1)}, u32[]{:S(2)}) copy-start(bf16[128,4096]{1,0:T(8,128)(2,1)} %param.11) | copy-start | bytes 3145732
  113.8 10.1 %all-to-all-start.2 = ((bf16[8,16,512]{2,1,0:T(8,128)(2,1)}), bf16[8,16,512]{2,1,0:T(8,128)(2,1)S(1)}, u32[]{:S(2)}, u32[]{:S(2)}) async-start(bf16[8,16,512]{2,1,0:T(8,128)(2,1)} %fusion.10), calls=%async_computation.2 | async-start | bytes 262144 | tf_op jit(solution)/shard_map/gated_back_to_rows/all_to_all | solution.py:104
  117.2 81.8 %all-gather.5.cloned.1.call-start = ((), (), s32[]{:S(2)}) async-start(), calls=%async_computation.5 | async-start | bytes 4325376 | tf_op jit(solution)/shard_map/output_projection/all_gather | solution.py:107
  123.9 0.7 copy-start.4
Sparse Core Ops, SparseCore 0:
  9.1 76.4 all-gather.2
  124.7 74.2 all-gather.4
